TPU v7x, 512 devices: a whole 4x8x8 slice. The times are simulated.
512 devices in a mesh: ctx: 64 (over x, z, core), head: 8 (over y).
Axes of the slice: x: 4, y: 8, z: 8, core: 2. Of those that a mesh axis runs over, the one named last changes fastest.
Arguments:
- query_rows: bfloat16 [65536, 1024], P('ctx', 'head'), may hold values from -8 to 8
- key_rows: bfloat16 [65536, 1024], P('ctx', 'head'), may hold values from -8 to 8
- value_rows: bfloat16 [65536, 1024], P('ctx', 'head'), may hold values from -6 to 6
- out_grad: bfloat16 [65536, 1024], P('ctx', 'head'), may hold values from -6 to 6
- out_weight: bfloat16 [1024, 1024], P('head'), may hold values from -0.1875 to 0.1875
- neighbours: int32 [512, 12], replicated, may hold values from 0 to 511, as said below
- counts: int32 [512], replicated, may hold values from 3 to 12, as said below
Outputs:
- query_grad: bfloat16 [65536, 1024], P('ctx', 'head')
- key_grad: bfloat16 [65536, 1024], P('ctx', 'head')
- value_grad: bfloat16 [65536, 1024], P('ctx', 'head')
- weight_grad: float32 [1024, 1024], P('head')
Inputs may be any that keep to these rules, and one draw needn't show every extreme that they name: `neighbours`: row g names block g in slot 0, then distinct blocks held by ctx indices g // 8 - 1 to g // 8 + 1; slots 1 and 2 include a block of each of the ctx indices g // 8 - 1 and g // 8 + 1 that exists; slots from counts[g] on hold g again. `counts`: block 0 uses all 12 slots.
All inputs are finite; a program needn't handle non-finite values.
Results may differ from a plain program's by a relative error of at most 0.012.
The roundings to bfloat16 on the way count: a program that leaves them out, or rounds other values in their place, can miss the bound.
Values may be sent and summed in bfloat16 or wider, within the bound.
No kernel may reach another device: no remote copies, remote signals or barrier semaphores. Data moves between devices by JAX's collectives and lax.ppermute only.
A program may use at most 64 MiB of HBM per device.

v0:
```python
import jax
import jax.numpy as jnp
from jax import lax
from jax.sharding import PartitionSpec as P

HD = 64
BS = 128


def with_halo(cells, sides, width):
    for axis, dim in sides:
        count = lax.axis_size(axis)
        ends = count - 1
        head = lax.slice_in_dim(cells, 0, width, axis=dim)
        tail = lax.slice_in_dim(cells, cells.shape[dim] - width, cells.shape[dim], axis=dim)
        cells = jnp.concatenate(
            [
                lax.ppermute(tail, axis, [(i, (i + 1) % count) for i in range(ends)]),
                cells,
                lax.ppermute(head, axis, [((i + 1) % count, i) for i in range(ends)]),
            ],
            axis=dim,
        )
    return cells


def shifted(x, axis, by):
    count = lax.axis_size(axis)
    pairs = [(i, i + by) for i in range(count) if 0 <= i + by < count]
    return lax.ppermute(x, axis, pairs)


def head_scores(query_block, key_block, factor):
    return (
        jnp.einsum("qhd,khd->hqk", query_block, key_block, preferred_element_type=jnp.float32)
        * factor
    )


def masked_scores(query_block, key_block, usable, factor):
    key_mask = jnp.repeat(usable, key_block.shape[0] // usable.shape[0])
    return jnp.where(key_mask[None, None, :], head_scores(query_block, key_block, factor), -1e30)


def padded_forward(query_block, key_block, value_block, usable, factor):
    scores = masked_scores(query_block, key_block, usable, factor)
    highest = jnp.max(scores, axis=2)
    log_total = highest + jnp.log(jnp.sum(jnp.exp(scores - highest[:, :, None]), axis=2))
    soft_weights = jnp.exp(scores - log_total[:, :, None]).astype(jnp.bfloat16)
    attended = jnp.einsum(
        "hqk,khd->qhd", soft_weights, value_block, preferred_element_type=jnp.float32
    )
    return (attended.astype(jnp.bfloat16), log_total)


def pair_backward(
    query_block, grad_block, log_total, dot_block, key_block, value_block, usable, factor
):
    scores = masked_scores(query_block, key_block, usable, factor)
    soft_full = jnp.exp(scores - log_total[:, :, None])
    grad_weights = jnp.einsum(
        "qhd,khd->hqk", grad_block, value_block, preferred_element_type=jnp.float32
    )
    grad_scores = (soft_full * (grad_weights - dot_block[:, :, None])).astype(jnp.bfloat16)
    grad_query = (
        jnp.einsum("hqk,khd->qhd", grad_scores, key_block, preferred_element_type=jnp.float32)
        * factor
    )
    grad_key = (
        jnp.einsum("hqk,qhd->khd", grad_scores, query_block, preferred_element_type=jnp.float32)
        * factor
    )
    grad_value = jnp.einsum(
        "hqk,qhd->khd",
        soft_full.astype(jnp.bfloat16),
        grad_block,
        preferred_element_type=jnp.float32,
    )
    return (grad_query, grad_key, grad_value)


def body(query_rows, key_rows, value_rows, out_grad, out_weight, neighbours, counts):
    row_count, col_count = query_rows.shape
    head_count = col_count // HD
    blocks = row_count // BS
    extent = 3 * blocks
    slot_total = neighbours.shape[1]
    block_total = counts.shape[0]
    factor = HD ** (-0.5)
    ctx_index = lax.axis_index("ctx")
    offset = (ctx_index - 1) * blocks
    packed = jnp.concatenate([key_rows, value_rows], axis=1)
    window = with_halo(packed, (("ctx", 0),), row_count)
    window = window.reshape(extent, BS, 2 * col_count)
    slot_ids = jnp.arange(slot_total, dtype=jnp.int32)
    query_blocks = query_rows.reshape(blocks, BS, head_count, HD)

    def fetch_all(places):
        picked = window[places]
        key_block = picked[:, :, :col_count].reshape(slot_total * BS, head_count, HD)
        value_block = picked[:, :, col_count:].reshape(slot_total * BS, head_count, HD)
        return (key_block, value_block)

    def slot_table(block_id):
        inside = (block_id >= 0) & (block_id < block_total)
        clamped = jnp.clip(block_id, 0, block_total - 1)
        relative = neighbours[clamped] - offset
        places = jnp.clip(relative, 0, extent - 1)
        active = jnp.where(inside, counts[clamped], 0)
        return (relative, places, active)

    def forward_block(block_index):
        relative, places, active = slot_table(ctx_index * blocks + block_index)
        query_block = query_blocks[block_index]
        key_block, value_block = fetch_all(places)
        return padded_forward(query_block, key_block, value_block, slot_ids < active, factor)

    attended_blocks, log_totals = lax.map(forward_block, jnp.arange(blocks, dtype=jnp.int32))
    attended = attended_blocks.reshape(row_count, col_count)
    shard_piece = lax.all_gather(out_grad, "head", axis=1, tiled=True)
    grad_sum = jnp.einsum("ro,jo->rj", shard_piece, out_weight, preferred_element_type=jnp.float32)
    product = jnp.einsum("rj,ro->jo", attended, shard_piece, preferred_element_type=jnp.float32)
    weight_sum = product
    grad_sum, weight_sum = (grad_sum, weight_sum)
    node_count = row_count * lax.axis_size("ctx")
    weight_grad = lax.psum(weight_sum, "ctx") * node_count ** (-0.5)
    grad_attended = grad_sum.astype(jnp.bfloat16)
    grad_blocks = grad_attended.reshape(blocks, BS, head_count, HD)
    row_dots = jnp.sum(
        grad_blocks.astype(jnp.float32) * attended_blocks.astype(jnp.float32), axis=3
    ).transpose(0, 2, 1)

    def sweep_step(totals, block_index):
        relative, places, active = slot_table(ctx_index * blocks + block_index)
        query_block = query_blocks[block_index]
        grad_block = grad_blocks[block_index]
        log_total = log_totals[block_index]
        dot_block = row_dots[block_index]
        key_block, value_block = fetch_all(places)
        grad_query, grad_key, grad_value = pair_backward(
            query_block,
            grad_block,
            log_total,
            dot_block,
            key_block,
            value_block,
            slot_ids < active,
            factor,
        )
        update = jnp.concatenate(
            [
                grad_key.reshape(slot_total, BS, col_count),
                grad_value.reshape(slot_total, BS, col_count),
            ],
            axis=2,
        )
        totals = totals.at[places].add(jnp.where((slot_ids < active)[:, None, None], update, 0.0))
        return (totals, grad_query.astype(jnp.bfloat16))

    blank_totals = jnp.zeros((extent, BS, 2 * col_count), jnp.float32)
    totals, grad_queries = lax.scan(sweep_step, blank_totals, jnp.arange(blocks, dtype=jnp.int32))
    middle = totals[blocks : 2 * blocks]
    from_right = shifted(totals[:blocks], "ctx", -1)
    from_left = shifted(totals[2 * blocks :], "ctx", 1)
    combined = middle + from_right + from_left
    query_grad = grad_queries.reshape(row_count, col_count)
    key_grad = combined[:, :, :col_count].reshape(row_count, col_count).astype(jnp.bfloat16)
    value_grad = combined[:, :, col_count:].reshape(row_count, col_count).astype(jnp.bfloat16)
    return (query_grad, key_grad, value_grad, weight_grad)


def solution(mesh):
    placed = (
        P("ctx", "head"),
        P("ctx", "head"),
        P("ctx", "head"),
        P("ctx", "head"),
        P("head", None),
        P(),
        P(),
    )
    return jax.shard_map(
        body,
        mesh=mesh,
        in_specs=placed,
        out_specs=(P("ctx", "head"), P("ctx", "head"), P("ctx", "head"), P("head", None)),
        check_vma=False,
    )
```

profile of v0, /device:TPU:8, one launch (start us, length us, event | category | flops | bytes accessed | tf_op | source)
XLA Modules:
  0.0 513.1 jit_solution(8677155265565717120)
XLA Ops:
  9.3 1.3 collective-permute-start.1
  10.6 3.8 collective-permute-start
  14.6 1.6 copy.63
  18.2 1.3 pad_maximum_fusion
  20.3 81.6 %while.30 = (s32[]{:T(128)}, bf16[8,128,2,64]{1,3,2,0:T(8,128)(2,1)}, f32[8,2,128]{2,1,0:T(2,128)S(1)}, s32[8]{0:T(128)S(1)}, s32[]{:T(128)}, /*index=5*/s32[512...) while((s32[]{:T(128)}, ...), condition=%wide.region_3.4_spmd.clone, body=%wide.region_0.3_spmd.clone.sunk | while | flops 103433040 | bytes 11877893 | solution.py:118
  27.7 1.3 fusion.85
  37.9 1.3 fusion.85
  48.1 1.3 fusion.85
  58.3 1.3 fusion.85
  68.5 1.3 fusion.85
  78.7 1.3 fusion.85
  88.9 1.3 fusion.85
  99.1 1.3 fusion.85
  101.9 2.3 convolution_convert_fusion.1
  106.1 2.0 broadcast_in_dim.88
  108.1 176.7 %while.31 = (s32[]{:T(128)}, f32[24,128,256]{2,1,0:T(8,128)}, bf16[8,128,2,64]{1,3,2,0:T(8,128)(2,1)}, s32[8]{0:T(128)S(1)}, s32[]{:T(128)}, /*index=5*/s32[512,...) while((s32[]{:T(128)}, f32[24,128,256]{2,1,0:T(8,128)}, ...), condition=%wide.region_7.8_spmd.clone, body=%wide.region_5.7_spmd.clone.sunk | while | flops 255820880 | bytes 43038368 | solution.py:161
  115.7 1.3 fusion.100
  116.9 1.2 fusion.101
  122.4 1.4 maximum_select_fusion.2
  123.9 1.7 copy.91
  125.6 4.7 scatter_fusion
  137.8 1.3 fusion.100
  139.1 1.2 fusion.101
  144.6 1.4 maximum_select_fusion.2
  146.0 1.7 copy.91
  147.7 4.5 scatter_fusion
  159.8 1.3 fusion.100
  161.1 1.2 fusion.101
  166.6 1.4 maximum_select_fusion.2
  168.1 1.7 copy.91
  169.8 4.8 scatter_fusion
  182.1 1.3 fusion.100
  183.3 1.2 fusion.101
  188.9 1.4 maximum_select_fusion.2
  190.3 1.7 copy.91
  192.0 4.5 scatter_fusion
  204.0 1.3 fusion.100
  205.3 1.2 fusion.101
  210.8 1.4 maximum_select_fusion.2
  212.3 1.7 copy.91
  214.0 4.5 scatter_fusion
  226.0 1.3 fusion.100
  227.3 1.2 fusion.101
  232.8 1.4 maximum_select_fusion.2
  234.2 1.7 copy.91
  235.9 4.8 scatter_fusion
  248.3 1.3 fusion.100
  249.5 1.2 fusion.101
  255.0 1.4 maximum_select_fusion.2
  256.5 1.7 copy.91
  258.2 4.4 scatter_fusion
  270.2 1.3 fusion.100
  271.4 1.2 fusion.101
  277.0 1.4 maximum_select_fusion.2
  278.4 1.7 copy.91
  280.1 4.7 scatter_fusion
  284.8 3.2 fusion.46
  288.1 1.3 collective-permute-start.2
  289.4 5.9 %collective-permute-start.3 = (f32[8,128,256]{2,1,0:T(8,128)}, f32[8,128,256]{2,1,0:T(8,128)S(1)}, u32[]{:S(2)}, u32[]{:S(2)}) collective-permute-start(f32[8,128,256]{2,1,0:T(8,128)} %get-tuple-element.506), channel_id=1, source_target_pairs={{0,8},{8,16},{16,24},{24,32},{32,40},{40,48},{48,56},{56,64},{64,7... | collective-permute-start | bytes 3145736 | tf_op jit(solution)/shard_map/ppermute | solution.py:30
  295.4 1.2 fusion.40
  296.7 1.3 copy.70
  298.9 203.1 %all-reduce.2.cloned.1.call-done = f32[128,1024]{1,0:T(8,128)} async-done(((f32[128,1024]{1,0:T(8,128)}), f32[128,1024]{1,0:T(8,128)}) %all-reduce.2.cloned.1.call-update) | async-done | bytes 524304 | tf_op jit(solution)/shard_map/psum | solution.py:126
  502.0 1.9 broadcast_multiply_fusion
  503.9 1.4 add_convert_fusion
  (343 shorter events, 122.9 us)
Async XLA Ops:
  7.2 94.7 %copy-start = (bf16[128,1024]{1,0:T(8,128)(2,1)S(1)}, bf16[128,1024]{1,0:T(8,128)(2,1)}, u32[]{:S(2)}) copy-start(bf16[128,1024]{1,0:T(8,128)(2,1)} %param.15) | copy-start | bytes 786436
  7.2 9.0 %copy-start.7 = (bf16[1024,128]{1,0:T(8,128)(2,1)S(1)}, bf16[1024,128]{1,0:T(8,128)(2,1)}, u32[]{:S(2)}) copy-start(bf16[1024,128]{1,0:T(8,128)(2,1)} %param.11) | copy-start | bytes 786436
  7.2 94.7 %all-gather.2.cloned.1.call-start = ((), (), s32[]{:S(2)}) async-start(), calls=%async_computation | async-start | bytes 2359296 | tf_op jit(solution)/shard_map/all_gather | solution.py:120
  9.3 8.1 %collective-permute-start.1 = (bf16[1024,256]{1,0:T(8,128)(2,1)S(1)}, bf16[1024,256]{1,0:T(8,128)(2,1)S(1)}, u32[]{:S(2)}, u32[]{:S(2)}) collective-permute-start(bf16[1024,256]{1,0:T(8,128)(2,1)S(1)} %constant_dynamic-update-slice_fusion), channel_id=1, source_target_pairs={{8,0},{16,8},{24,16},{32,24},{40,32},{48,40},{56,48},{64,56},{72,6... | collective-permute-start | bytes 1572872 | tf_op jit(solution)/shard_map/ppermute | solution.py:20
  10.6 7.6 %collective-permute-start = (bf16[1024,256]{1,0:T(8,128)(2,1)S(1)}, bf16[1024,256]{1,0:T(8,128)(2,1)}, u32[]{:S(2)}, u32[]{:S(2)}) collective-permute-start(bf16[1024,256]{1,0:T(8,128)(2,1)S(1)} %constant_dynamic-update-slice_fusion), channel_id=1, source_target_pairs={{0,8},{8,16},{16,24},{24,32},{32,40},{40,48},{48,56},{56,64},{64,7... | collective-permute-start | bytes 1572872 | tf_op jit(solution)/shard_map/ppermute | solution.py:18
  14.5 487.5 %all-reduce.2.cloned.1.call-start = ((), (), s32[]{:S(2)}) async-start(), calls=%async_computation.1 | async-start | bytes 1048576 | tf_op jit(solution)/shard_map/psum | solution.py:126
  17.4 2.9 copy-start.8
  17.4 0.8 copy-start.6
  101.9 3.3 copy-start.4
  108.1 6.1 %copy-start.1 = (bf16[24,128,256]{2,1,0:T(8,128)(2,1)}, bf16[24,128,256]{2,1,0:T(8,128)(2,1)S(1)}, u32[]{:S(2)}) copy-start(bf16[24,128,256]{2,1,0:T(8,128)(2,1)S(1)} %get-tuple-element.755) | copy-start | bytes 4718596 | tf_op jit(solution)/shard_map/while
  125.6 4.7 copy-start.2
  130.3 6.1 %copy-start.1 = (bf16[24,128,256]{2,1,0:T(8,128)(2,1)}, bf16[24,128,256]{2,1,0:T(8,128)(2,1)S(1)}, u32[]{:S(2)}) copy-start(bf16[24,128,256]{2,1,0:T(8,128)(2,1)S(1)} %get-tuple-element.755) | copy-start | bytes 4718596 | tf_op jit(solution)/shard_map/while
  147.7 4.5 copy-start.2
  152.3 6.1 %copy-start.1 = (bf16[24,128,256]{2,1,0:T(8,128)(2,1)}, bf16[24,128,256]{2,1,0:T(8,128)(2,1)S(1)}, u32[]{:S(2)}) copy-start(bf16[24,128,256]{2,1,0:T(8,128)(2,1)S(1)} %get-tuple-element.755) | copy-start | bytes 4718596 | tf_op jit(solution)/shard_map/while
  169.8 4.8 copy-start.2
  174.5 6.1 %copy-start.1 = (bf16[24,128,256]{2,1,0:T(8,128)(2,1)}, bf16[24,128,256]{2,1,0:T(8,128)(2,1)S(1)}, u32[]{:S(2)}) copy-start(bf16[24,128,256]{2,1,0:T(8,128)(2,1)S(1)} %get-tuple-element.755) | copy-start | bytes 4718596 | tf_op jit(solution)/shard_map/while
  192.0 4.5 copy-start.2
  196.5 6.1 %copy-start.1 = (bf16[24,128,256]{2,1,0:T(8,128)(2,1)}, bf16[24,128,256]{2,1,0:T(8,128)(2,1)S(1)}, u32[]{:S(2)}) copy-start(bf16[24,128,256]{2,1,0:T(8,128)(2,1)S(1)} %get-tuple-element.755) | copy-start | bytes 4718596 | tf_op jit(solution)/shard_map/while
  214.0 4.5 copy-start.2
  218.4 6.1 %copy-start.1 = (bf16[24,128,256]{2,1,0:T(8,128)(2,1)}, bf16[24,128,256]{2,1,0:T(8,128)(2,1)S(1)}, u32[]{:S(2)}) copy-start(bf16[24,128,256]{2,1,0:T(8,128)(2,1)S(1)} %get-tuple-element.755) | copy-start | bytes 4718596 | tf_op jit(solution)/shard_map/while
  235.9 4.8 copy-start.2
  240.7 6.1 %copy-start.1 = (bf16[24,128,256]{2,1,0:T(8,128)(2,1)}, bf16[24,128,256]{2,1,0:T(8,128)(2,1)S(1)}, u32[]{:S(2)}) copy-start(bf16[24,128,256]{2,1,0:T(8,128)(2,1)S(1)} %get-tuple-element.755) | copy-start | bytes 4718596 | tf_op jit(solution)/shard_map/while
  258.2 4.4 copy-start.2
  262.6 6.1 %copy-start.1 = (bf16[24,128,256]{2,1,0:T(8,128)(2,1)}, bf16[24,128,256]{2,1,0:T(8,128)(2,1)S(1)}, u32[]{:S(2)}) copy-start(bf16[24,128,256]{2,1,0:T(8,128)(2,1)S(1)} %get-tuple-element.755) | copy-start | bytes 4718596 | tf_op jit(solution)/shard_map/while
  280.1 4.7 copy-start.2
  284.8 10.4 %copy-start.5 = (bf16[8,128,2,64]{1,3,2,0:T(8,128)(2,1)S(1)}, bf16[8,128,2,64]{1,3,2,0:T(8,128)(2,1)}, u32[]{:S(2)}) copy-start(bf16[8,128,2,64]{1,3,2,0:T(8,128)(2,1)} %get-tuple-element.294) | copy-start | bytes 786436
  284.8 10.6 %copy-start.3 = (bf16[1024,1024]{1,0:T(8,128)(2,1)S(1)}, bf16[1024,1024]{1,0:T(8,128)(2,1)}, u32[]{:S(2)}) copy-start(bf16[1024,1024]{1,0:T(8,128)(2,1)} %all-gather.2.cloned.1.call-done) | copy-start | bytes 6291460
  288.1 215.8 %collective-permute-start.2 = (f32[8,128,256]{2,1,0:T(8,128)}, f32[8,128,256]{2,1,0:T(8,128)S(1)}, u32[]{:S(2)}, u32[]{:S(2)}) collective-permute-start(f32[8,128,256]{2,1,0:T(8,128)} %get-tuple-element.505), channel_id=1, source_target_pairs={{8,0},{16,8},{24,16},{32,24},{40,32},{48,40},{56,48},{64,56},{72,6... | collective-permute-start | bytes 3145736 | tf_op jit(solution)/shard_map/ppermute | solution.py:30
  289.4 214.6 %collective-permute-start.3 = (f32[8,128,256]{2,1,0:T(8,128)}, f32[8,128,256]{2,1,0:T(8,128)S(1)}, u32[]{:S(2)}, u32[]{:S(2)}) collective-permute-start(f32[8,128,256]{2,1,0:T(8,128)} %get-tuple-element.506), channel_id=1, source_target_pairs={{0,8},{8,16},{16,24},{24,32},{32,40},{40,48},{48,56},{56,64},{64,7... | collective-permute-start | bytes 3145736 | tf_op jit(solution)/shard_map/ppermute | solution.py:30
Sparse Core Ops, SparseCore 0:
  14.6 56.4 all-gather.1
  296.8 205.1 all-reduce.1
where the time goes:
time: 518 us; the launch traced here: 513 us
  waiting for transfers between devices  203 us (39%)
  local copies, waits for them, and re-layouts  96.8 us (19%)
  other arithmetic  67.7 us (13%)
  matrix products  66.1 us (13%)
  loops' own time  52.9 us (10%)
  between operations  14.2 us (3%)
  starting transfers between devices  12.4 us (2%)
    psum x1, waiting for transfers between devices, body(): weight_grad = lax.psum(weight_sum, 'ctx') * node_count ** (-0.5)  203 us
    scatter-add x8, other arithmetic, sweep_step(): totals.at[places]  36.9 us
    another operation x1, loops' own time, body(): lax.map(forward_block, jnp.arange(blocks, dtype=jnp.int32))  26.5 us
    another operation x1, loops' own time, body(): lax.scan(sweep_step, blank_totals, jnp.arange(blocks, dtype=jnp.int32))  26.4 us
    dot_general x16, matrix products, head_scores(): jnp.einsum('qhd,khd->hqk', query_block, key_block, preferred_element_type...  20.1 us
    select_n x8, local copies, waits for them, and re-layouts, sweep_step(): jnp.where((slot_ids < active)[:, None, None], update, 0.0)  13.6 us
    select_n x8, other arithmetic, sweep_step(): jnp.where((slot_ids < active)[:, None, None], update, 0.0)  11.5 us
  transfers between devices with their start and end apart: 6, of which 1 were waited for; matrix products, arithmetic and copies ran while one was open for 13% of the time, Pallas kernels for 0%

commit v1 on v0

--- a/solution.py
+++ b/solution.py
@@ -2,9 +2,15 @@
 import jax.numpy as jnp
 from jax import lax
 from jax.sharding import PartitionSpec as P
+from jax.lax import all_gather
 
 HD = 64
 BS = 128
+
+
+def bring_values_for(block_in):
+    block_out = all_gather(block_in, axis_name="ctx")
+    return jnp.sum(block_out, axis=0)
 
 
 def with_halo(cells, sides, width):
@@ -123,7 +129,7 @@
     weight_sum = product
     grad_sum, weight_sum = (grad_sum, weight_sum)
     node_count = row_count * lax.axis_size("ctx")
-    weight_grad = lax.psum(weight_sum, "ctx") * node_count ** (-0.5)
+    weight_grad = bring_values_for(weight_sum) * node_count ** (-0.5)
     grad_attended = grad_sum.astype(jnp.bfloat16)
     grad_blocks = grad_attended.reshape(blocks, BS, head_count, HD)
     row_dots = jnp.sum(

time: 518 us -> 416 us (0.80)
  the two profiles are of different devices: /device:TPU:8 before, /device:TPU:46 now
where the time goes in v1:
time: 416 us; the launch traced here: 411 us
  local copies, waits for them, and re-layouts  150 us (36%)
  other arithmetic  81.2 us (20%)
  matrix products  73 us (18%)
  loops' own time  53.3 us (13%)
  starting transfers between devices  20 us (5%)
  waiting for transfers between devices  18.7 us (4%)
  between operations  14.2 us (3%)
    scatter-add x8, other arithmetic, sweep_step(): totals.at[places]  36.9 us
    slice x24, local copies, waits for them, and re-layouts, fetch_all(): picked[:, :, col_count:].reshape(slot_total * BS, head_count, HD)  28.8 us
    another operation x1, loops' own time, body(): lax.scan(sweep_step, blank_totals, jnp.arange(blocks, dtype=jnp.int32))  27.2 us
    another operation x1, loops' own time, body(): lax.map(forward_block, jnp.arange(blocks, dtype=jnp.int32))  26.1 us
    dot_general x16, matrix products, head_scores(): jnp.einsum('qhd,khd->hqk', query_block, key_block, preferred_element_type...  22.5 us
    reshape x16, local copies, waits for them, and re-layouts, fetch_all(): picked[:, :, col_count:].reshape(slot_total * BS, head_count, HD)  18.6 us
    dot_general x8, matrix products, padded_forward(): jnp.einsum('hqk,khd->qhd', soft_weights, value_block, preferred_element_t...  16.6 us
    ppermute x2, waiting for transfers between devices, shifted(): return lax.ppermute(x, axis, pairs)  15.1 us
  transfers between devices with their start and end apart: 6, of which 4 were waited for; matrix products, arithmetic and copies ran while one was open for 70% of the time, Pallas kernels for 0%

profile of v1, /device:TPU:46, one launch (start us, length us, event | category | flops | bytes accessed | tf_op | source)
XLA Modules:
  0.0 410.7 jit_solution(6168499971818952287)
XLA Ops:
  9.3 1.9 collective-permute-start
  11.2 10.7 %collective-permute-start.1 = (bf16[1024,256]{1,0:T(8,128)(2,1)S(1)}, bf16[1024,256]{1,0:T(8,128)(2,1)}, u32[]{:S(2)}, u32[]{:S(2)}) collective-permute-start(bf16[1024,256]{1,0:T(8,128)(2,1)S(1)} %constant_dynamic-update-slice_fusion), channel_id=1, source_target_pairs={{8,0},{16,8},{24,16},{32,24},{40,32},{48,40},{56,48},{64,56},{72,6... | collective-permute-start | bytes 1572872 | tf_op jit(solution)/shard_map/ppermute | solution.py:26
  25.0 1.8 collective-permute-done
  26.8 1.8 collective-permute-done.1
  30.5 131.9 %while.30 = (s32[]{:T(128)}, bf16[8,128,2,64]{1,3,2,0:T(8,128)(2,1)}, f32[8,2,128]{2,1,0:T(2,128)S(1)}, s32[8]{0:T(128)S(1)}, s32[]{:T(128)}, /*index=5*/s32[512...) while((s32[]{:T(128)}, ...), condition=%wide.region_3.4_spmd.clone, body=%wide.region_0.3_spmd.clone.sunk | while | flops 103433040 | bytes 11878393 | solution.py:124
  40.6 2.2 copy.87
  42.8 2.1 reshape.214
  44.9 2.1 fusion.86
  55.2 1.5 fusion.85
  57.1 2.2 copy.87
  59.3 2.1 reshape.214
  61.4 2.1 fusion.86
  73.6 2.2 copy.87
  75.8 2.1 reshape.214
  77.9 2.1 fusion.86
  90.1 2.2 copy.87
  92.3 2.1 reshape.214
  94.4 2.1 fusion.86
  106.6 2.2 copy.87
  108.8 2.1 reshape.214
  110.9 2.1 fusion.86
  123.1 2.2 copy.87
  125.3 2.1 reshape.214
  127.3 2.1 fusion.86
  139.6 2.2 copy.87
  141.8 2.1 reshape.214
  143.8 2.1 fusion.86
  156.1 2.2 copy.87
  158.3 2.1 reshape.214
  160.3 2.1 fusion.86
  163.5 2.8 fusion.40
  166.4 2.3 convolution_convert_fusion.1
  169.9 2.0 broadcast_in_dim.88
  171.9 190.0 %while.31 = (s32[]{:T(128)}, f32[24,128,256]{2,1,0:T(8,128)}, bf16[8,128,2,64]{1,3,2,0:T(8,128)(2,1)S(1)}, s32[8]{0:T(128)S(1)}, s32[]{:T(128)}, /*index=5*/s32[...) while((s32[]{:T(128)}, f32[24,128,256]{2,1,0:T(8,128)}, ...), condition=%wide.region_7.8_spmd.clone, body=%wide.region_5.7_spmd.clone.sunk | while | flops 255820880 | bytes 47757036 | solution.py:167
  187.2 1.8 maximum_select_fusion.2
  188.9 1.7 copy.91
  190.6 4.6 %scatter_fusion = f32[24,128,256]{2,1,0:T(8,128)} fusion(f32[24,128,256]{2,1,0:T(8,128)} %get-tuple-element.729, s32[12]{0:T(128)S(1)} %fusion.97, f32[12,128,256]{2,1,0:T(8,128)} %copy.91), kind=kCustom, calls=%fused_computation.2.clone.clone.1 | custom fusion | flops 393216 | bytes 4718640 | tf_op jit(solution)/shard_map/while/body/eval_jaxpr/scatter-add | solution.py:163
  210.9 1.8 maximum_select_fusion.2
  212.7 1.7 copy.91
  214.3 4.4 %scatter_fusion = f32[24,128,256]{2,1,0:T(8,128)} fusion(f32[24,128,256]{2,1,0:T(8,128)} %get-tuple-element.729, s32[12]{0:T(128)S(1)} %fusion.97, f32[12,128,256]{2,1,0:T(8,128)} %copy.91), kind=kCustom, calls=%fused_computation.2.clone.clone.1 | custom fusion | flops 393216 | bytes 4718640 | tf_op jit(solution)/shard_map/while/body/eval_jaxpr/scatter-add | solution.py:163
  234.4 1.9 maximum_select_fusion.2
  236.3 1.7 copy.91
  238.0 4.7 %scatter_fusion = f32[24,128,256]{2,1,0:T(8,128)} fusion(f32[24,128,256]{2,1,0:T(8,128)} %get-tuple-element.729, s32[12]{0:T(128)S(1)} %fusion.97, f32[12,128,256]{2,1,0:T(8,128)} %copy.91), kind=kCustom, calls=%fused_computation.2.clone.clone.1 | custom fusion | flops 393216 | bytes 4718640 | tf_op jit(solution)/shard_map/while/body/eval_jaxpr/scatter-add | solution.py:163
  258.4 1.8 maximum_select_fusion.2
  260.2 1.7 copy.91
  261.9 4.8 %scatter_fusion = f32[24,128,256]{2,1,0:T(8,128)} fusion(f32[24,128,256]{2,1,0:T(8,128)} %get-tuple-element.729, s32[12]{0:T(128)S(1)} %fusion.97, f32[12,128,256]{2,1,0:T(8,128)} %copy.91), kind=kCustom, calls=%fused_computation.2.clone.clone.1 | custom fusion | flops 393216 | bytes 4718640 | tf_op jit(solution)/shard_map/while/body/eval_jaxpr/scatter-add | solution.py:163
  282.3 1.9 maximum_select_fusion.2
  284.2 1.7 copy.91
  285.9 4.5 %scatter_fusion = f32[24,128,256]{2,1,0:T(8,128)} fusion(f32[24,128,256]{2,1,0:T(8,128)} %get-tuple-element.729, s32[12]{0:T(128)S(1)} %fusion.97, f32[12,128,256]{2,1,0:T(8,128)} %copy.91), kind=kCustom, calls=%fused_computation.2.clone.clone.1 | custom fusion | flops 393216 | bytes 4718640 | tf_op jit(solution)/shard_map/while/body/eval_jaxpr/scatter-add | solution.py:163
  306.0 1.8 maximum_select_fusion.2
  307.8 1.7 copy.91
  309.5 4.8 %scatter_fusion = f32[24,128,256]{2,1,0:T(8,128)} fusion(f32[24,128,256]{2,1,0:T(8,128)} %get-tuple-element.729, s32[12]{0:T(128)S(1)} %fusion.97, f32[12,128,256]{2,1,0:T(8,128)} %copy.91), kind=kCustom, calls=%fused_computation.2.clone.clone.1 | custom fusion | flops 393216 | bytes 4718640 | tf_op jit(solution)/shard_map/while/body/eval_jaxpr/scatter-add | solution.py:163
  329.9 1.8 maximum_select_fusion.2
  331.7 1.7 copy.91
  333.4 4.4 %scatter_fusion = f32[24,128,256]{2,1,0:T(8,128)} fusion(f32[24,128,256]{2,1,0:T(8,128)} %get-tuple-element.729, s32[12]{0:T(128)S(1)} %fusion.97, f32[12,128,256]{2,1,0:T(8,128)} %copy.91), kind=kCustom, calls=%fused_computation.2.clone.clone.1 | custom fusion | flops 393216 | bytes 4718640 | tf_op jit(solution)/shard_map/while/body/eval_jaxpr/scatter-add | solution.py:163
  353.4 1.8 maximum_select_fusion.2
  355.2 1.7 copy.91
  356.9 4.7 %scatter_fusion = f32[24,128,256]{2,1,0:T(8,128)} fusion(f32[24,128,256]{2,1,0:T(8,128)} %get-tuple-element.729, s32[12]{0:T(128)S(1)} %fusion.97, f32[12,128,256]{2,1,0:T(8,128)} %copy.91), kind=kCustom, calls=%fused_computation.2.clone.clone.1 | custom fusion | flops 393216 | bytes 4718640 | tf_op jit(solution)/shard_map/while/body/eval_jaxpr/scatter-add | solution.py:163
  362.0 3.1 fusion.46
  365.0 5.4 %collective-permute-start.2 = (f32[8,128,256]{2,1,0:T(8,128)}, f32[8,128,256]{2,1,0:T(8,128)S(1)}, u32[]{:S(2)}, u32[]{:S(2)}) collective-permute-start(f32[8,128,256]{2,1,0:T(8,128)} %get-tuple-element.505), channel_id=1, source_target_pairs={{8,0},{16,8},{24,16},{32,24},{40,32},{48,40},{56,48},{64,56},{72,6... | collective-permute-start | bytes 3145736 | tf_op jit(solution)/shard_map/ppermute | solution.py:36
  370.5 1.9 collective-permute-start.3
  373.7 9.3 %collective-permute-done.2 = f32[8,128,256]{2,1,0:T(8,128)S(1)} collective-permute-done((f32[8,128,256]{2,1,0:T(8,128)}, f32[8,128,256]{2,1,0:T(8,128)S(1)}, u32[]{:S(2)}, u32[]{:S(2)}) %collective-permute-start.2) | collective-permute-done | bytes 1048608 | tf_op jit(solution)/shard_map/ppermute | solution.py:36
  383.1 5.8 %collective-permute-done.3 = f32[8,128,256]{2,1,0:T(8,128)S(1)} collective-permute-done((f32[8,128,256]{2,1,0:T(8,128)}, f32[8,128,256]{2,1,0:T(8,128)S(1)}, u32[]{:S(2)}, u32[]{:S(2)}) %collective-permute-start.3) | collective-permute-done | bytes 1048608 | tf_op jit(solution)/shard_map/ppermute | solution.py:36
  391.2 11.8 %reduce_sum.30 = f32[128,1024]{1,0:T(8,128)S(1)} reduce(f32[64,128,1024]{2,1,0:T(8,128)} %bitcast.152, f32[]{:T(128)} %constant.121.clone.1), dimensions={0}, to_apply=%region_8.9 | reduce | flops 8257536 | bytes 34078724 | tf_op jit(solution)/shard_map/reduce_sum | solution.py:13
  (388 shorter events, 165.8 us)
Async XLA Ops:
  7.2 159.2 %copy-start = (bf16[128,1024]{1,0:T(8,128)(2,1)S(1)}, bf16[128,1024]{1,0:T(8,128)(2,1)}, u32[]{:S(2)}) copy-start(bf16[128,1024]{1,0:T(8,128)(2,1)} %param.15) | copy-start | bytes 786436
  7.2 17.0 %copy-start.8 = (s32[512,12]{0,1:T(8,128)S(1)}, s32[512,12]{0,1:T(8,128)}, u32[]{:S(2)}) copy-start(s32[512,12]{0,1:T(8,128)} %param.16) | copy-start | bytes 73732
  7.2 156.3 %all-gather.4.cloned.1.call-start = ((), (), s32[]{:S(2)}) async-start(), calls=%async_computation | async-start | bytes 2359296 | tf_op jit(solution)/shard_map/all_gather | solution.py:126
  9.3 17.5 %collective-permute-start = (bf16[1024,256]{1,0:T(8,128)(2,1)S(1)}, bf16[1024,256]{1,0:T(8,128)(2,1)S(1)}, u32[]{:S(2)}, u32[]{:S(2)}) collective-permute-start(bf16[1024,256]{1,0:T(8,128)(2,1)S(1)} %constant_dynamic-update-slice_fusion), channel_id=1, source_target_pairs={{0,8},{8,16},{16,24},{24,32},{32,40},{40,48},{48,56},{56,64},{64,7... | collective-permute-start | bytes 1572872 | tf_op jit(solution)/shard_map/ppermute | solution.py:24
  11.2 17.3 %collective-permute-start.1 = (bf16[1024,256]{1,0:T(8,128)(2,1)S(1)}, bf16[1024,256]{1,0:T(8,128)(2,1)}, u32[]{:S(2)}, u32[]{:S(2)}) collective-permute-start(bf16[1024,256]{1,0:T(8,128)(2,1)S(1)} %constant_dynamic-update-slice_fusion), channel_id=1, source_target_pairs={{8,0},{16,8},{24,16},{32,24},{40,32},{48,40},{56,48},{64,56},{72,6... | collective-permute-start | bytes 1572872 | tf_op jit(solution)/shard_map/ppermute | solution.py:26
  21.9 369.3 %all-gather.6.cloned.1.call-start = ((), (), s32[]{:S(2)}) async-start(), calls=%async_computation.1 | async-start | bytes 34078720 | tf_op jit(solution)/shard_map/all_gather | solution.py:12
  25.0 5.5 %copy-start.9 = (s32[512]{0:T(512)S(1)}, s32[512]{0:T(512)}, u32[]{:S(2)}) copy-start(s32[512]{0:T(512)} %param.17) | copy-start | bytes 6148
  166.4 3.3 copy-start.7
  171.9 6.9 %copy-start.2 = (bf16[24,128,256]{2,1,0:T(8,128)(2,1)}, bf16[24,128,256]{2,1,0:T(8,128)(2,1)S(1)}, u32[]{:S(2)}) copy-start(bf16[24,128,256]{2,1,0:T(8,128)(2,1)S(1)} %get-tuple-element.755) | copy-start | bytes 4718596 | tf_op jit(solution)/shard_map/while
  179.3 1.6 copy-start.6
  179.6 2.1 copy-start.4
  190.6 4.6 %copy-start.5 = (bf16[1536,2,64]{0,2,1:T(8,128)(2,1)S(1)}, bf16[1536,2,64]{0,2,1:T(8,128)(2,1)}, u32[]{:S(2)}) copy-start(bf16[1536,2,64]{0,2,1:T(8,128)(2,1)} %copy-done.4) | copy-start | bytes 1179652 | tf_op jit(solution)/shard_map/while
  190.6 5.0 %copy-start.3 = (bf16[24,128,256]{2,1,0:T(8,128)(2,1)S(1)}, bf16[24,128,256]{2,1,0:T(8,128)(2,1)}, u32[]{:S(2)}) copy-start(bf16[24,128,256]{2,1,0:T(8,128)(2,1)} %copy-done.2) | copy-start | bytes 4718596 | tf_op jit(solution)/shard_map/while
  195.7 6.9 %copy-start.2 = (bf16[24,128,256]{2,1,0:T(8,128)(2,1)}, bf16[24,128,256]{2,1,0:T(8,128)(2,1)S(1)}, u32[]{:S(2)}) copy-start(bf16[24,128,256]{2,1,0:T(8,128)(2,1)S(1)} %get-tuple-element.755) | copy-start | bytes 4718596 | tf_op jit(solution)/shard_map/while
  203.0 1.6 copy-start.6
  203.3 2.1 copy-start.4
  214.3 4.4 %copy-start.5 = (bf16[1536,2,64]{0,2,1:T(8,128)(2,1)S(1)}, bf16[1536,2,64]{0,2,1:T(8,128)(2,1)}, u32[]{:S(2)}) copy-start(bf16[1536,2,64]{0,2,1:T(8,128)(2,1)} %copy-done.4) | copy-start | bytes 1179652 | tf_op jit(solution)/shard_map/while
  214.3 4.8 %copy-start.3 = (bf16[24,128,256]{2,1,0:T(8,128)(2,1)S(1)}, bf16[24,128,256]{2,1,0:T(8,128)(2,1)}, u32[]{:S(2)}) copy-start(bf16[24,128,256]{2,1,0:T(8,128)(2,1)} %copy-done.2) | copy-start | bytes 4718596 | tf_op jit(solution)/shard_map/while
  219.2 6.9 %copy-start.2 = (bf16[24,128,256]{2,1,0:T(8,128)(2,1)}, bf16[24,128,256]{2,1,0:T(8,128)(2,1)S(1)}, u32[]{:S(2)}) copy-start(bf16[24,128,256]{2,1,0:T(8,128)(2,1)S(1)} %get-tuple-element.755) | copy-start | bytes 4718596 | tf_op jit(solution)/shard_map/while
  226.6 1.6 copy-start.6
  226.8 2.1 copy-start.4
  238.0 4.7 %copy-start.5 = (bf16[1536,2,64]{0,2,1:T(8,128)(2,1)S(1)}, bf16[1536,2,64]{0,2,1:T(8,128)(2,1)}, u32[]{:S(2)}) copy-start(bf16[1536,2,64]{0,2,1:T(8,128)(2,1)} %copy-done.4) | copy-start | bytes 1179652 | tf_op jit(solution)/shard_map/while
  238.0 5.1 %copy-start.3 = (bf16[24,128,256]{2,1,0:T(8,128)(2,1)S(1)}, bf16[24,128,256]{2,1,0:T(8,128)(2,1)}, u32[]{:S(2)}) copy-start(bf16[24,128,256]{2,1,0:T(8,128)(2,1)} %copy-done.2) | copy-start | bytes 4718596 | tf_op jit(solution)/shard_map/while
  243.1 7.0 %copy-start.2 = (bf16[24,128,256]{2,1,0:T(8,128)(2,1)}, bf16[24,128,256]{2,1,0:T(8,128)(2,1)S(1)}, u32[]{:S(2)}) copy-start(bf16[24,128,256]{2,1,0:T(8,128)(2,1)S(1)} %get-tuple-element.755) | copy-start | bytes 4718596 | tf_op jit(solution)/shard_map/while
  250.5 1.6 copy-start.6
  250.8 2.1 copy-start.4
  261.9 4.8 %copy-start.5 = (bf16[1536,2,64]{0,2,1:T(8,128)(2,1)S(1)}, bf16[1536,2,64]{0,2,1:T(8,128)(2,1)}, u32[]{:S(2)}) copy-start(bf16[1536,2,64]{0,2,1:T(8,128)(2,1)} %copy-done.4) | copy-start | bytes 1179652 | tf_op jit(solution)/shard_map/while
  261.9 5.2 %copy-start.3 = (bf16[24,128,256]{2,1,0:T(8,128)(2,1)S(1)}, bf16[24,128,256]{2,1,0:T(8,128)(2,1)}, u32[]{:S(2)}) copy-start(bf16[24,128,256]{2,1,0:T(8,128)(2,1)} %copy-done.2) | copy-start | bytes 4718596 | tf_op jit(solution)/shard_map/while
  267.1 6.9 %copy-start.2 = (bf16[24,128,256]{2,1,0:T(8,128)(2,1)}, bf16[24,128,256]{2,1,0:T(8,128)(2,1)S(1)}, u32[]{:S(2)}) copy-start(bf16[24,128,256]{2,1,0:T(8,128)(2,1)S(1)} %get-tuple-element.755) | copy-start | bytes 4718596 | tf_op jit(solution)/shard_map/while
  274.4 1.6 copy-start.6
  274.7 2.1 copy-start.4
  285.9 4.5 %copy-start.5 = (bf16[1536,2,64]{0,2,1:T(8,128)(2,1)S(1)}, bf16[1536,2,64]{0,2,1:T(8,128)(2,1)}, u32[]{:S(2)}) copy-start(bf16[1536,2,64]{0,2,1:T(8,128)(2,1)} %copy-done.4) | copy-start | bytes 1179652 | tf_op jit(solution)/shard_map/while
  285.9 4.9 %copy-start.3 = (bf16[24,128,256]{2,1,0:T(8,128)(2,1)S(1)}, bf16[24,128,256]{2,1,0:T(8,128)(2,1)}, u32[]{:S(2)}) copy-start(bf16[24,128,256]{2,1,0:T(8,128)(2,1)} %copy-done.2) | copy-start | bytes 4718596 | tf_op jit(solution)/shard_map/while
  290.8 6.9 %copy-start.2 = (bf16[24,128,256]{2,1,0:T(8,128)(2,1)}, bf16[24,128,256]{2,1,0:T(8,128)(2,1)S(1)}, u32[]{:S(2)}) copy-start(bf16[24,128,256]{2,1,0:T(8,128)(2,1)S(1)} %get-tuple-element.755) | copy-start | bytes 4718596 | tf_op jit(solution)/shard_map/while
  298.2 1.6 copy-start.6
  298.5 2.1 copy-start.4
  309.5 4.8 %copy-start.5 = (bf16[1536,2,64]{0,2,1:T(8,128)(2,1)S(1)}, bf16[1536,2,64]{0,2,1:T(8,128)(2,1)}, u32[]{:S(2)}) copy-start(bf16[1536,2,64]{0,2,1:T(8,128)(2,1)} %copy-done.4) | copy-start | bytes 1179652 | tf_op jit(solution)/shard_map/while
  309.5 5.2 %copy-start.3 = (bf16[24,128,256]{2,1,0:T(8,128)(2,1)S(1)}, bf16[24,128,256]{2,1,0:T(8,128)(2,1)}, u32[]{:S(2)}) copy-start(bf16[24,128,256]{2,1,0:T(8,128)(2,1)} %copy-done.2) | copy-start | bytes 4718596 | tf_op jit(solution)/shard_map/while
  314.7 6.9 %copy-start.2 = (bf16[24,128,256]{2,1,0:T(8,128)(2,1)}, bf16[24,128,256]{2,1,0:T(8,128)(2,1)S(1)}, u32[]{:S(2)}) copy-start(bf16[24,128,256]{2,1,0:T(8,128)(2,1)S(1)} %get-tuple-element.755) | copy-start | bytes 4718596 | tf_op jit(solution)/shard_map/while
  322.1 1.6 copy-start.6
  322.4 2.1 copy-start.4
  333.4 4.4 %copy-start.5 = (bf16[1536,2,64]{0,2,1:T(8,128)(2,1)S(1)}, bf16[1536,2,64]{0,2,1:T(8,128)(2,1)}, u32[]{:S(2)}) copy-start(bf16[1536,2,64]{0,2,1:T(8,128)(2,1)} %copy-done.4) | copy-start | bytes 1179652 | tf_op jit(solution)/shard_map/while
  333.4 4.8 %copy-start.3 = (bf16[24,128,256]{2,1,0:T(8,128)(2,1)S(1)}, bf16[24,128,256]{2,1,0:T(8,128)(2,1)}, u32[]{:S(2)}) copy-start(bf16[24,128,256]{2,1,0:T(8,128)(2,1)} %copy-done.2) | copy-start | bytes 4718596 | tf_op jit(solution)/shard_map/while
  338.2 6.9 %copy-start.2 = (bf16[24,128,256]{2,1,0:T(8,128)(2,1)}, bf16[24,128,256]{2,1,0:T(8,128)(2,1)S(1)}, u32[]{:S(2)}) copy-start(bf16[24,128,256]{2,1,0:T(8,128)(2,1)S(1)} %get-tuple-element.755) | copy-start | bytes 4718596 | tf_op jit(solution)/shard_map/while
  345.6 1.6 copy-start.6
  345.9 2.1 copy-start.4
  356.9 4.7 %copy-start.5 = (bf16[1536,2,64]{0,2,1:T(8,128)(2,1)S(1)}, bf16[1536,2,64]{0,2,1:T(8,128)(2,1)}, u32[]{:S(2)}) copy-start(bf16[1536,2,64]{0,2,1:T(8,128)(2,1)} %copy-done.4) | copy-start | bytes 1179652 | tf_op jit(solution)/shard_map/while
  356.9 5.1 %copy-start.3 = (bf16[24,128,256]{2,1,0:T(8,128)(2,1)S(1)}, bf16[24,128,256]{2,1,0:T(8,128)(2,1)}, u32[]{:S(2)}) copy-start(bf16[24,128,256]{2,1,0:T(8,128)(2,1)} %copy-done.2) | copy-start | bytes 4718596 | tf_op jit(solution)/shard_map/while
  365.0 18.0 %collective-permute-start.2 = (f32[8,128,256]{2,1,0:T(8,128)}, f32[8,128,256]{2,1,0:T(8,128)S(1)}, u32[]{:S(2)}, u32[]{:S(2)}) collective-permute-start(f32[8,128,256]{2,1,0:T(8,128)} %get-tuple-element.505), channel_id=1, source_target_pairs={{8,0},{16,8},{24,16},{32,24},{40,32},{48,40},{56,48},{64,56},{72,6... | collective-permute-start | bytes 3145736 | tf_op jit(solution)/shard_map/ppermute | solution.py:36
  370.5 18.4 %collective-permute-start.3 = (f32[8,128,256]{2,1,0:T(8,128)}, f32[8,128,256]{2,1,0:T(8,128)S(1)}, u32[]{:S(2)}, u32[]{:S(2)}) collective-permute-start(f32[8,128,256]{2,1,0:T(8,128)} %get-tuple-element.506), channel_id=1, source_target_pairs={{0,8},{8,16},{16,24},{24,32},{32,40},{40,48},{48,56},{56,64},{64,7... | collective-permute-start | bytes 3145736 | tf_op jit(solution)/shard_map/ppermute | solution.py:36
  391.2 12.6 %copy-start.1 = (bf16[128,1024]{1,0:T(8,128)(2,1)S(1)}, bf16[128,1024]{1,0:T(8,128)(2,1)}, u32[]{:S(2)}) copy-start(bf16[128,1024]{1,0:T(8,128)(2,1)} %param.15) | copy-start | bytes 786436
Sparse Core Ops, SparseCore 0:
  22.0 46.8 all-gather.3
  166.5 145.0 all-gather.5
